TPU v7x, 256 devices: a whole 4x4x8 slice. The times are simulated.
256 devices in a mesh: grp: 2 (over core), gx: 16 (over y, z_lo), gy: 8 (over z_hi, x).
Axes of the slice: x: 4, y: 4, z: 8 (z_hi: 2, z_lo: 4; z = z_hi * 4 + z_lo), core: 2. Of those that a mesh axis runs over, the one named last changes fastest.
Arguments:
- source: float32 [128, 256, 256], P('gx', 'gy', 'grp'), may hold values from -8 to 8
- fill: int32 [128, 256, 256], P('gx', 'gy', 'grp'), may hold values 0 or 1
- material: int32 [128, 256, 256], P('gx', 'gy', 'grp'), may hold values from 0 to 7
- thickness: float32 [128, 256], P('gx', 'gy'), may hold values from 0.7 to 1.3
- perm_table: float32 [8], replicated, may hold values from 0.2 to 2
- stiff_table: float32 [8], replicated, may hold values from 0.5 to 2
Outputs:
- pressure: float32 [128, 256, 256], P('gx', 'gy', 'grp')
- displacement: float32 [128, 256, 256], P('gx', 'gy', 'grp')
- thickness_out: float32 [128, 256], P('gx', 'gy')
All inputs are finite; a program needn't handle non-finite values. No bound on the sum of `fill` on one device may be relied on, other than what follows from the above.
Results may differ from a plain program's by a relative error of at most 0.0003.
Values sent between devices are 32-bit elements; how exact they have to be, the bound alone decides.
A program may use at most 128 MiB of HBM per device.

v0:
```python
import jax
import jax.numpy as jnp
from jax import lax
from jax.experimental import pallas as pl
from jax.experimental.pallas import tpu as pltpu
from jax.sharding import PartitionSpec as P

STEPS = 2
W = 4
MESH = pl.DeviceIdType.MESH
DIRS = [(-1, -1), (-1, 0), (-1, 1), (0, -1), (0, 1), (1, -1), (1, 0), (1, 1)]
UNROLL = 2


def spread(table, material, count):
    total = jnp.zeros(material.shape, jnp.float32)
    for entry in range(count):
        total = jnp.where(material == entry, table[entry], total)
    return total


def make_kernel(nx, ny, nz, ngx, ngy, mats):
    rows, depth = ny // 2, 2 * nz
    ex, ey = nx + 2 * W, rows + 2 * W
    nslab = 2 * ngy
    levels = depth.bit_length() - 1
    x_from = {-1: (W, W), 0: (W, nx), 1: (nx, W)}
    x_to = {-1: (W + nx, W), 0: (W, nx), 1: (0, W)}
    y_from = {-1: (0, W), 0: (0, rows), 1: (rows - W, W)}
    y_to = {-1: (rows, W), 0: (0, rows), 1: (rows + W, W)}

    def kernel(source, fill, material, thickness, perm, stiffs, p_out, d_out, th_out,
               s_ext, f_ext, k_ext, px0, px1, px2, ta, tb, mat, gx_, gy_, gz_, a_,
               alpha, gamma, inv, wts, cols, fin_p, fin_d, fin_t,
               send, recv, psend, precv, loc):
        g = lax.axis_index("grp")
        ix = lax.axis_index("gx")
        slab = 2 * lax.axis_index("gy") + g
        other = 1 - g

        def place(dx, dy):
            x = jnp.clip(ix + dx, 0, ngx - 1)
            s = jnp.clip(slab + dy, 0, nslab - 1)
            return {"grp": lax.rem(s, 2), "gx": x, "gy": lax.div(s, 2)}

        def there(dx, dy):
            ok = jnp.int32(1)
            if dx == -1:
                ok = ok * jnp.where(ix > 0, 1, 0)
            if dx == 1:
                ok = ok * jnp.where(ix < ngx - 1, 1, 0)
            if dy == -1:
                ok = ok * jnp.where(slab > 0, 1, 0)
            if dy == 1:
                ok = ok * jnp.where(slab < nslab - 1, 1, 0)
            return ok

        alive = [there(*d) for d in DIRS]

        barrier = pltpu.get_barrier_semaphore()
        for i, d in enumerate(DIRS):
            @pl.when(alive[i] == 1)
            def _():
                pl.semaphore_signal(barrier, 1, device_id=place(*d), device_id_type=MESH)
        pl.semaphore_wait(barrier, sum(alive))

        mine = pl.multiple_of(g * rows, rows)
        theirs = pl.multiple_of(other * rows, rows)
        z_here = pl.multiple_of(g * nz, nz)
        z_there = pl.multiple_of(other * nz, nz)
        own_x, own_y = pl.ds(W, nx), pl.ds(0, rows)

        def trade(n, ref, dst):
            out = pltpu.make_async_remote_copy(
                ref.at[:, pl.ds(theirs, rows), :], dst.at[own_x, own_y, pl.ds(z_here, nz)],
                psend.at[n], precv.at[n], device_id={"grp": other}, device_id_type=MESH)
            keep = pltpu.make_async_copy(
                ref.at[:, pl.ds(mine, rows), :], dst.at[own_x, own_y, pl.ds(z_here, nz)], loc.at[n])
            return out, keep

        trades = [trade(0, source, s_ext), trade(1, fill, f_ext), trade(2, material, mat)]
        for out, keep in trades:
            out.start()
            keep.start()

        def hop(e, ref, i):
            dx, dy = DIRS[i]
            if ref is cols:
                src = ref.at[1, pl.ds(*y_from[dy]), :]
                dst = ref.at[1 - dx, pl.ds(*y_to[dy]), :]
            else:
                src = ref.at[pl.ds(*x_from[dx]), pl.ds(*y_from[dy]), :]
                dst = ref.at[pl.ds(*x_to[dx]), pl.ds(*y_to[dy]), :]
            return pltpu.make_async_remote_copy(
                src, dst, send.at[e, i], recv.at[e, i], device_id=place(dx, dy), device_id_type=MESH)

        def push(e, ref):
            for i in range(8):
                @pl.when(alive[i] == 1)
                def _():
                    hop(e, ref, i).start()

        def arrive(e, ref):
            for i in range(8):
                @pl.when(alive[7 - i] == 1)
                def _():
                    hop(e, ref, i).wait_recv()

        def sent(e, ref):
            for i in range(8):
                @pl.when(alive[i] == 1)
                def _():
                    hop(e, ref, i).wait_send()

        lane = lax.broadcasted_iota(jnp.int32, (rows, 128), 1)
        pick_row = lax.broadcasted_iota(jnp.int32, (rows, ny), 1) == (
            lax.broadcasted_iota(jnp.int32, (rows, ny), 0) + g * rows)

        def column_of(x):
            line = jnp.broadcast_to(thickness[pl.ds(x, 1), :], (rows, ny))
            return jnp.sum(jnp.where(pick_row, line, 0.0), axis=1, keepdims=True)

        th = jnp.zeros((rows, 128), jnp.float32)
        for x in range(nx):
            th = jnp.where(lane == x, column_of(x), th)

        for n, ref in ((0, s_ext), (1, f_ext)):
            trades[n][0].wait_recv()
            trades[n][1].wait()
            push(n, ref)
        trades[2][0].wait_recv()
        trades[2][1].wait()

        for x in range(nx):
            t = th[:, x:x + 1]
            k_ext[W + x, 0:rows, :] = spread(perm, mat[W + x, 0:rows, :], mats) * (t * t * t)
        push(2, k_ext)

        for i in range(8):
            dx, dy = DIRS[i]
            x0, xn = x_to[-dx]
            y0, yn = y_to[-dy]

            @pl.when(alive[i] == 0)
            def _():
                s_ext[x0:x0 + xn, y0:y0 + yn, :] = jnp.zeros((xn, yn, depth), jnp.float32)
                f_ext[x0:x0 + xn, y0:y0 + yn, :] = jnp.zeros((xn, yn, depth), jnp.int32)
                k_ext[x0:x0 + xn, y0:y0 + yn, :] = jnp.zeros((xn, yn, depth), jnp.float32)
                for ref in (px0, px1, px2):
                    ref[x0:x0 + xn, y0:y0 + yn, :] = jnp.zeros((xn, yn, depth), jnp.float32)
                cols[1 + dx, y0:y0 + yn, :] = jnp.zeros((yn, 128), jnp.float32)

        zpos = lax.broadcasted_iota(jnp.int32, (rows, depth), 1)

        def reduce_columns(x, carry):
            fl = f_ext[W + x, 0:rows, :].astype(jnp.float32)
            st = spread(stiffs, mat[W + x, 0:rows, :], mats) * (1.0 - 0.5 * fl)
            low = jnp.where(zpos == 0, 0.0, pltpu.roll(st, 1, 1))
            high = jnp.where(zpos == depth - 1, 0.0, pltpu.roll(st, depth - 1, 1))
            up = 0.5 * (st + high)
            down = 0.5 * (st + low)
            a = jnp.where(zpos == 0, 0.0, down)
            c = jnp.where(zpos == depth - 1, 0.0, up)
            e = 0.001 * st + jnp.where(zpos == 0, down, 0.0) + jnp.where(zpos == depth - 1, up, 0.0)
            r = jnp.full((rows, depth), 0.001 / depth, jnp.float32)
            for level in range(levels):
                stride = 1 << level
                back = depth - stride
                recip = 1.0 / (a + c + e)
                al = a * pltpu.roll(recip, stride, 1)
                ga = c * pltpu.roll(recip, back, 1)
                alpha[level, x] = al
                gamma[level, x] = ga
                a = al * pltpu.roll(a, stride, 1)
                c = ga * pltpu.roll(c, back, 1)
                e = e + al * pltpu.roll(e, stride, 1) + ga * pltpu.roll(e, back, 1)
                r = r + al * pltpu.roll(r, stride, 1) + ga * pltpu.roll(r, back, 1)
            recip = 1.0 / e
            inv[x] = recip
            wts[x] = r * recip
            return carry

        lax.fori_loop(0, nx, reduce_columns, 0)

        zfull = lax.broadcasted_iota(jnp.int32, (ey, depth), 1)

        def faces(x, carry):
            k = k_ext[x]
            front = jnp.where(zfull == 0, 0.0, pltpu.roll(k, 1, 1))
            back = jnp.where(zfull == depth - 1, 0.0, pltpu.roll(k, depth - 1, 1))
            gzp = 0.5 * (k + back)
            gzm = 0.5 * (k + front)
            gyp = 0.5 * (k + pltpu.roll(k, ey - 1, 0))
            gym = 0.5 * (k + pltpu.roll(k, 1, 0))
            gxp = 0.5 * (k + k_ext[x + 1])
            gxm = 0.5 * (k + k_ext[x - 1])
            fl = f_ext[x].astype(jnp.float32)
            denom = gxp + gxm + gyp + gym + gzp + gzm + 1.0 - fl
            gx_[x] = gxp
            gy_[x] = gyp
            gz_[x] = jnp.where(zfull == depth - 1, 0.0, gzp)
            a_[x] = fl / denom
            return carry

        def all_faces():
            gx_[0] = 0.5 * (k_ext[0] + k_ext[1])
            lax.fori_loop(1, ex - 1, faces, 0)

        def relax(src, dst, level, width):
            def one(x, carry):
                here = src[x]
                gy = gy_[x]
                gz = gz_[x]
                total = s_ext[x] + gx_[x] * src[x + 1] + gx_[x - 1] * src[x - 1]
                total = total + gy * pltpu.roll(here, ey - 1, 0) + pltpu.roll(gy * here, 1, 0)
                total = total + gz * pltpu.roll(here, depth - 1, 1) + pltpu.roll(gz * here, 1, 1)
                value = a_[x] * total
                if width == ey:
                    dst[x] = value
                elif dst is fin_p:
                    dst[x - W] = value[0:width]
                else:
                    dst[x, 0:width] = value[0:width]
                return carry

            lax.fori_loop(level, ex - level, one, 0, unroll=UNROLL)

        def first(x, carry):
            ta[x] = a_[x] * s_ext[x]
            return carry

        def mean_factor(held, base):
            comp = jnp.zeros((rows, 128), jnp.float32)
            for x in range(nx):
                part = wts[x] * (1.0 - held[base + x, 0:rows, :])
                comp = jnp.where(lane == x, jnp.sum(part, axis=1, keepdims=True), comp)
            return 1.0 + 0.3 * jnp.tanh(comp)

        arrive(2, k_ext)
        arrive(1, f_ext)
        all_faces()
        arrive(0, s_ext)
        lax.fori_loop(1, ex - 1, first, 0)
        relax(ta, tb, 2, ey)
        relax(tb, ta, 3, ey)
        relax(ta, px0, 4, rows)
        push(3, px0)
        arrive(3, px0)
        relax(px0, ta, 1, ey)
        relax(ta, tb, 2, ey)
        relax(tb, ta, 3, ey)
        relax(ta, px1, 4, rows)

        factor = mean_factor(px1, W)
        cols[1, 0:rows, :] = factor
        push(5, cols)
        push(4, px1)
        th = th * factor
        arrive(5, cols)
        sent(2, k_ext)
        for x in range(ex):
            part, pos = (0, x + nx - W) if x < W else ((1, x - W) if x < W + nx else (2, x - W - nx))
            t = cols[part, :, pos:pos + 1]
            k_ext[x] = k_ext[x] * (t * t * t)
        all_faces()
        arrive(4, px1)
        relax(px1, ta, 1, ey)
        relax(ta, tb, 2, ey)
        relax(tb, ta, 3, ey)
        relax(ta, px2, 4, rows)
        push(6, px2)
        arrive(6, px2)
        relax(px2, ta, 1, ey)
        relax(ta, tb, 2, ey)
        relax(tb, ta, 3, ey)
        relax(ta, fin_p, 4, rows)

        def give(n, ref, dst):
            out = pltpu.make_async_remote_copy(
                ref.at[:, :, pl.ds(z_there, nz)], dst.at[:, pl.ds(mine, rows), :],
                psend.at[n], precv.at[n], device_id={"grp": other}, device_id_type=MESH)
            keep = pltpu.make_async_copy(
                ref.at[:, :, pl.ds(z_here, nz)], dst.at[:, pl.ds(mine, rows), :], loc.at[n])
            return out, keep

        gives = [give(3, fin_p, p_out), give(4, fin_d, d_out)]
        for c in gives[0]:
            c.start()

        def solve_columns(x, carry):
            r = 0.001 * (1.0 - fin_p[x])
            for level in range(levels):
                stride = 1 << level
                r = (r + alpha[level, x] * pltpu.roll(r, stride, 1)
                     + gamma[level, x] * pltpu.roll(r, depth - stride, 1))
            fin_d[x] = r * inv[x]
            return carry

        lax.fori_loop(0, nx, solve_columns, 0, unroll=2)
        for c in gives[1]:
            c.start()
        fin_t[...] = th * mean_factor(fin_p, 0)
        t_out = pltpu.make_async_remote_copy(
            fin_t, th_out.at[pl.ds(mine, rows), :], psend.at[5], precv.at[5],
            device_id={"grp": other}, device_id_type=MESH)
        t_keep = pltpu.make_async_copy(fin_t, th_out.at[pl.ds(mine, rows), :], loc.at[5])
        t_out.start()
        t_keep.start()

        for e, ref in ((0, s_ext), (1, f_ext), (3, px0), (4, px1), (5, cols), (6, px2)):
            sent(e, ref)
        for out, keep in trades:
            out.wait_send()
        for out, keep in gives + [(t_out, t_keep)]:
            out.wait_send()
            out.wait_recv()
            keep.wait()

    return kernel, rows, depth, ex, ey, levels


def body(source, fill, material, thickness, perm_table, stiff_table):
    nx, ny, nz = source.shape
    kernel, rows, depth, ex, ey, levels = make_kernel(
        nx, ny, nz, lax.axis_size("gx"), lax.axis_size("gy"), perm_table.shape[0])
    f32, i32 = jnp.float32, jnp.int32
    vm, sm = pl.BlockSpec(memory_space=pltpu.VMEM), pl.BlockSpec(memory_space=pltpu.SMEM)
    ext = pltpu.VMEM((ex, ey, depth), f32)
    iext = pltpu.VMEM((ex, ey, depth), i32)
    own = pltpu.VMEM((nx, rows, depth), f32)
    pressure, disp, thick = pl.pallas_call(
        kernel,
        out_shape=(
            jax.ShapeDtypeStruct((nx, ny, nz), f32),
            jax.ShapeDtypeStruct((nx, ny, nz), f32),
            jax.ShapeDtypeStruct((ny, 128), f32),
        ),
        in_specs=[vm, vm, vm, vm, sm, sm],
        out_specs=(vm, vm, vm),
        scratch_shapes=[
            ext, iext, ext, ext, ext, ext, ext, ext, iext, ext, ext, ext, ext,
            pltpu.VMEM((levels, nx, rows, depth), f32),
            pltpu.VMEM((levels, nx, rows, depth), f32),
            own, own,
            pltpu.VMEM((3, ey, 128), f32),
            own, own,
            pltpu.VMEM((rows, 128), f32),
            pltpu.SemaphoreType.DMA((7, 8)),
            pltpu.SemaphoreType.DMA((7, 8)),
            pltpu.SemaphoreType.DMA((6,)),
            pltpu.SemaphoreType.DMA((6,)),
            pltpu.SemaphoreType.DMA((6,)),
        ],
        compiler_params=pltpu.CompilerParams(collective_id=0, has_side_effects=True),
    )(source, fill, material, thickness, perm_table, stiff_table)
    return pressure, disp, thick[:, :nx].T


def solution(mesh):
    return jax.shard_map(
        body,
        mesh=mesh,
        in_specs=(
            P("gx", "gy", "grp"),
            P("gx", "gy", "grp"),
            P("gx", "gy", "grp"),
            P("gx", "gy"),
            P(),
            P(),
        ),
        out_specs=(P("gx", "gy", "grp"), P("gx", "gy", "grp"), P("gx", "gy")),
        check_vma=False,
    )
```

profile of v0, /device:TPU:47, one launch (start us, length us, event | category | flops | bytes accessed | tf_op | source)
XLA Modules:
  0.0 69.3 jit_solution(12377876934559738128)
XLA Ops:
  0.6 65.0 %shard_map.85 = (f32[8,32,128]{2,1,0:T(8,128)}, f32[8,32,128]{2,1,0:T(8,128)}, f32[32,128]{1,0:T(8,128)}) custom-call(f32[8,32,128]{2,1,0:T(8,128)} %source.1, s32[8,32,128]{2,1,0:T(8,128)} %fill.1, s32[8,32,128]{2,1,0:T(8,128)} %material.1, f32[8,32]{1,0:T(8,128)} %thickness.1, f32[8]{0:T(128)} %perm.1, f32[8]{0:T(128)} %stiffs.1), custom_call_target="tpu_custom_call" | custom-call | tf_op jit(solution)/shard_map/pallas_call | solution.py:331
  65.7 0.7 %slice_bitcast_fusion = f32[8,32]{0,1:T(8,128)S(1)} fusion(f32[32,128]{1,0:T(8,128)} %get-tuple-element.8), kind=kLoop, calls=%fused_computation | loop fusion | bytes 2048 | tf_op jit(solution)/shard_map/transpose | solution.py:356
  66.4 0.7 copy.9
  67.1 0.0 copy-start
  67.1 1.6 %copy.12 = f32[8,32,128]{2,1,0:T(8,128)} copy(f32[8,32,128]{2,1,0:T(8,128)} %get-tuple-element.15) | data formatting | bytes 262144
  68.7 0.0 copy-done
  68.7 0.7 copy.13
Async XLA Ops:
  67.1 1.6 %copy-start = (f32[8,32,128]{2,1,0:T(8,128)S(1)}, f32[8,32,128]{2,1,0:T(8,128)}, u32[]{:S(2)}) copy-start(f32[8,32,128]{2,1,0:T(8,128)} %get-tuple-element.16) | copy-start | bytes 393220
where the time goes:
time: 69.5 us; the launch traced here: 69.3 us
  Pallas kernels  65 us (94%)
  local copies, waits for them, and re-layouts  3.64 us (5%)
    pallas_call x1, Pallas kernels, body(): pl.pallas_call(kernel, out_shape=(jax.ShapeDtypeStruct((nx, ny, nz), f32)...  65 us
    unnamed x5, local copies, waits for them, and re-layouts  2.92 us

commit v1 on v0

v1 whole, which is shorter than its diff:
```python
import jax
import jax.numpy as jnp
from jax import lax
from jax.experimental import pallas as pl
from jax.experimental.pallas import tpu as pltpu
from jax.sharding import PartitionSpec as P

W = 4
VMEM_LIMIT = 24 << 20
MESH = pl.DeviceIdType.MESH
DIRS = [(-1, -1), (-1, 0), (-1, 1), (0, -1), (0, 1), (1, -1), (1, 0), (1, 1)]
NINE = [(0, 0)] + DIRS
ORDER = [0, 1, 2, 3, 4, 5, 6, 7]
FACES = 2


def spread(table, material, count):
    total = jnp.zeros(material.shape, jnp.float32)
    for entry in range(count):
        total = jnp.where(material == entry, table[entry], total)
    return total


def make_kernel(nx, ny, nz, ngx, ngy, mats):
    rows, depth = ny // 2, 2 * nz
    ex, ey = nx + 2 * W, rows + 2 * W
    nslab = 2 * ngy
    levels = depth.bit_length() - 1

    def blocks(dx, dy, reach):
        xr = reach - abs(dy)
        yr = reach - abs(dx)
        xs, xd = {-1: ((0, xr), (W + nx, xr)), 0: ((0, nx), (W, nx)), 1: ((nx - xr, xr), (W - xr, xr))}[dx]
        ys, yd = {-1: ((0, yr), (rows, yr)), 0: ((0, rows), (0, rows)),
                  1: ((rows - yr, yr), (ey - yr, yr))}[dy]
        return xs, ys, xd, yd

    def kernel(source, fill, material, thickness, perm_table, stiff_table, p_out, d_out, th_out,
               s_ext, f_ext, k_ext, px0, px1, px2, ta, tb, gx_, gy_, gz_, a_,
               alpha, gamma, inv, wts, cols, fin_p, fin_d, mat, kloc, stloc, st, thick, line, line_in, perm, stiffs,
               csend, crecv, cloc, send, recv, psend, precv, loc):
        g = lax.axis_index("grp")
        ix = lax.axis_index("gx")
        iy = lax.axis_index("gy")
        slab = 2 * iy + g
        other = 1 - g

        def within(value, count):
            return jnp.where(value >= 0, 1, 0) * jnp.where(value < count, 1, 0)

        def place(dx, dy):
            x = jnp.clip(ix + dx, 0, ngx - 1)
            s = jnp.clip(slab + dy, 0, nslab - 1)
            return {"grp": lax.rem(s, 2), "gx": x, "gy": lax.div(s, 2)}

        alive = [within(ix + dx, ngx) * within(slab + dy, nslab) for dx, dy in DIRS]

        barrier = pltpu.get_barrier_semaphore()
        for dx in (-1, 0, 1):
            for dgy in (0, 2 * g - 1):
                for core in range(2):
                    ok = within(ix + dx, ngx) * within(iy + dgy, ngy)
                    if dx == 0 and isinstance(dgy, int):
                        ok = jnp.where(g == core, 0, 1)

                    @pl.when(ok == 1)
                    def _():
                        target = {"grp": core, "gx": jnp.clip(ix + dx, 0, ngx - 1),
                                  "gy": jnp.clip(iy + dgy, 0, ngy - 1)}
                        pl.semaphore_signal(barrier, 1, device_id=target, device_id_type=MESH)
        greeted = (sum(within(ix + dx, ngx) for dx in (-1, 0, 1))
                   * sum(within(2 * iy + j, nslab) for j in (-1, 0, 1, 2)) - 1)

        load_th = pltpu.make_async_copy(thickness, thick, loc.at[0])
        load_mat = pltpu.make_async_copy(material, mat, loc.at[1])
        load_perm = pltpu.make_async_copy(perm_table, perm, loc.at[6])
        load_stiff = pltpu.make_async_copy(stiff_table, stiffs, loc.at[7])
        for c in (load_th, load_mat, load_perm, load_stiff):
            c.start()

        for i in range(8):
            dx, dy = DIRS[i]
            _, _, (x0, xn), (y0, yn) = blocks(-dx, -dy, W)

            @pl.when(alive[i] == 0)
            def _():
                s_ext[x0:x0 + xn, y0:y0 + yn, :] = jnp.zeros((xn, yn, depth), jnp.float32)
                f_ext[x0:x0 + xn, y0:y0 + yn, :] = jnp.zeros((xn, yn, depth), jnp.int32)
                k_ext[x0:x0 + xn, y0:y0 + yn, :] = jnp.zeros((xn, yn, depth), jnp.float32)
                for ref in (px0, px1, px2):
                    ref[x0:x0 + xn, y0:y0 + yn, :] = jnp.zeros((xn, yn, depth), jnp.float32)
                cols[1 + dx, y0:y0 + yn, :] = jnp.zeros((yn, 128), jnp.float32)

        for c in (load_th, load_mat, load_perm, load_stiff):
            c.wait()
        diagonal = lax.broadcasted_iota(jnp.int32, (ny, ny), 0) == lax.broadcasted_iota(jnp.int32, (ny, ny), 1)
        for x in range(nx):
            across = jnp.broadcast_to(thick[x:x + 1, :], (ny, ny))
            t = jnp.sum(jnp.where(diagonal, across, 0.0), axis=1, keepdims=True)
            m = mat[x]
            kloc[x] = spread(perm, m, mats) * (t * t * t)
            stloc[x] = spread(stiffs, m, mats)

        pl.semaphore_wait(barrier, greeted)

        mine = pl.multiple_of(g * rows, rows)
        theirs = pl.multiple_of(other * rows, rows)
        z_here = pl.multiple_of(g * nz, nz)
        z_there = pl.multiple_of(other * nz, nz)
        consts = [(0, kloc, k_ext, W), (1, fill, f_ext, W - 1), (2, source, s_ext, W - 1)]

        def const_send(n, v, i, local=False):
            _, src, ext, reach = consts[n]
            dx, dy = NINE[i]
            (xs, xn), (ys, yn), (xd, _), (yd, _) = blocks(dx, dy, reach)
            core, dgy = (v + dy) % 2, (v + dy) // 2
            from_ = src.at[pl.ds(xs, xn), pl.ds(v * rows + ys, yn), :]
            to = ext.at[pl.ds(xd, xn), pl.ds(yd, yn), pl.ds(z_here, nz)]
            target = {"grp": core, "gx": jnp.clip(ix + dx, 0, ngx - 1), "gy": jnp.clip(iy + dgy, 0, ngy - 1)}
            if local:
                return pltpu.make_async_copy(from_, to, cloc.at[n, 0 if dy == 0 else 1])
            return pltpu.make_async_remote_copy(
                from_, to, csend.at[n, v, i], crecv.at[n, g, i], device_id=target, device_id_type=MESH)

        def const_each(group, do_away, do_keep):
            for v in range(2):
                for i in range(9):
                    dx, dy = NINE[i]
                    core, dgy = (v + dy) % 2, (v + dy) // 2
                    ok = within(ix + dx, ngx) * within(iy + dgy, ngy)
                    if dx == 0 and dgy == 0:
                        ok = jnp.where(g == core, 0, 1)
                        if do_keep is not None:
                            @pl.when(g == core)
                            def _():
                                for n in group:
                                    do_keep(const_send(n, v, i, True))

                    @pl.when(ok == 1)
                    def _():
                        for n in group:
                            do_away(const_send(n, v, i))

        def const_arrive(group):
            for src in range(2):
                for i in range(9):
                    dx, dy = NINE[i]
                    ok = within(ix - dx, ngx) * within(slab - dy, nslab)
                    if dx == 0:
                        here = jnp.where(g == src, 1, 0)
                        if dy == 1:
                            here = here * g
                        if dy == -1:
                            here = here * other
                        ok = ok * (1 - here)

                        @pl.when(here == 1)
                        def _():
                            for n in group:
                                _, ref, ext, reach = consts[n]
                                (xs, xn), (ys, yn), (xd, _), (yd, _) = blocks(dx, dy, reach)
                                pltpu.make_async_copy(
                                    ref.at[pl.ds(xs, xn), pl.ds(ys, yn), :],
                                    ext.at[pl.ds(xd, xn), pl.ds(yd, yn), pl.ds(src * nz, nz)],
                                    cloc.at[n, 0 if dy == 0 else 1]).wait()

                    @pl.when(ok == 1)
                    def _():
                        for n in group:
                            _, ref, ext, reach = consts[n]
                            (xs, xn), (ys, yn), (xd, _), (yd, _) = blocks(dx, dy, reach)
                            pltpu.make_async_remote_copy(
                                ref.at[pl.ds(xs, xn), pl.ds(ys, yn), :],
                                ext.at[pl.ds(xd, xn), pl.ds(yd, yn), pl.ds(src * nz, nz)],
                                csend.at[n, 0, i], crecv.at[n, src, i],
                                device_id={"grp": other}, device_id_type=MESH).wait_recv()

        st_away = pltpu.make_async_remote_copy(
            stloc.at[:, pl.ds(theirs, rows), :], st.at[:, :, pl.ds(z_here, nz)],
            psend.at[0], precv.at[0], device_id={"grp": other}, device_id_type=MESH)
        st_keep = pltpu.make_async_copy(
            stloc.at[:, pl.ds(mine, rows), :], st.at[:, :, pl.ds(z_here, nz)], loc.at[2])
        st_away.start()
        st_keep.start()
        for group in ((0, 1), (2,)):
            const_each(group, lambda c: c.start(), lambda c: c.start())

        def hop(e, ref, i):
            dx, dy = DIRS[i]
            (xs, xn), (ys, yn), (xd, _), (yd, _) = blocks(dx, dy, W)
            if ref is cols:
                src = ref.at[1, pl.ds(ys, yn), :]
                dst = ref.at[1 - dx, pl.ds(yd, yn), :]
            else:
                src = ref.at[pl.ds(W + xs, xn), pl.ds(ys, yn), :]
                dst = ref.at[pl.ds(xd, xn), pl.ds(yd, yn), :]
            return pltpu.make_async_remote_copy(
                src, dst, send.at[e, i], recv.at[e, i], device_id=place(dx, dy), device_id_type=MESH)

        def push(e, ref):
            for i in ORDER:
                @pl.when(alive[i] == 1)
                def _():
                    hop(e, ref, i).start()

        def arrive(e, ref):
            for i in range(8):
                @pl.when(alive[7 - i] == 1)
                def _():
                    hop(e, ref, i).wait_recv()

        def sent(e, ref):
            for i in range(8):
                @pl.when(alive[i] == 1)
                def _():
                    hop(e, ref, i).wait_send()

        zpos = lax.broadcasted_iota(jnp.int32, (rows, depth), 1)

        def reduce_columns(x, carry):
            s = st[x] * (1.0 - 0.5 * f_ext[W + x, 0:rows, :].astype(jnp.float32))
            low = jnp.where(zpos == 0, 0.0, pltpu.roll(s, 1, 1))
            high = jnp.where(zpos == depth - 1, 0.0, pltpu.roll(s, depth - 1, 1))
            up = 0.5 * (s + high)
            down = 0.5 * (s + low)
            a = jnp.where(zpos == 0, 0.0, down)
            c = jnp.where(zpos == depth - 1, 0.0, up)
            e = 0.001 * s + jnp.where(zpos == 0, down, 0.0) + jnp.where(zpos == depth - 1, up, 0.0)
            r = jnp.full((rows, depth), 0.001 / depth, jnp.float32)
            for level in range(levels):
                stride = 1 << level
                back = depth - stride
                recip = 1.0 / (a + c + e)
                al = a * pltpu.roll(recip, stride, 1)
                ga = c * pltpu.roll(recip, back, 1)
                alpha[level, x] = al
                gamma[level, x] = ga
                a = al * pltpu.roll(a, stride, 1)
                c = ga * pltpu.roll(c, back, 1)
                e = e + al * pltpu.roll(e, stride, 1) + ga * pltpu.roll(e, back, 1)
                r = r + al * pltpu.roll(r, stride, 1) + ga * pltpu.roll(r, back, 1)
            recip = 1.0 / e
            inv[x] = recip
            wts[x] = r * recip
            return carry

        zfull = lax.broadcasted_iota(jnp.int32, (ey, depth), 1)

        def faces(x, carry):
            k = k_ext[x]
            front = jnp.where(zfull == 0, 0.0, pltpu.roll(k, 1, 1))
            back = jnp.where(zfull == depth - 1, 0.0, pltpu.roll(k, depth - 1, 1))
            gzp = 0.5 * (k + back)
            gzm = 0.5 * (k + front)
            gyp = 0.5 * (k + pltpu.roll(k, ey - 1, 0))
            gym = 0.5 * (k + pltpu.roll(k, 1, 0))
            gxp = 0.5 * (k + k_ext[x + 1])
            gxm = 0.5 * (k + k_ext[x - 1])
            fl = f_ext[x].astype(jnp.float32)
            denom = gxp + gxm + gyp + gym + gzp + gzm + 1.0 - fl
            gx_[x] = gxp
            gy_[x] = gyp
            gz_[x] = jnp.where(zfull == depth - 1, 0.0, gzp)
            a_[x] = fl / denom
            return carry

        def all_faces():
            gx_[0] = 0.5 * (k_ext[0] + k_ext[1])
            lax.fori_loop(1, ex - 1, faces, 0, unroll=FACES)

        def relax(src, dst, level, width):
            def one(x, carry):
                here = src[x]
                gy = gy_[x]
                gz = gz_[x]
                total = s_ext[x] + gx_[x] * src[x + 1] + gx_[x - 1] * src[x - 1]
                total = total + gy * pltpu.roll(here, ey - 1, 0) + pltpu.roll(gy * here, 1, 0)
                total = total + gz * pltpu.roll(here, depth - 1, 1) + pltpu.roll(gz * here, 1, 1)
                value = a_[x] * total
                if width == ey:
                    dst[x] = value
                elif dst is fin_p:
                    dst[x - W] = value[0:width]
                else:
                    dst[x, 0:width] = value[0:width]
                return carry

            lax.fori_loop(level, ex - level, one, 0, unroll=ex - 2 * level)

        def first(x, carry):
            ta[x] = a_[x] * s_ext[x]
            return carry

        lane = lax.broadcasted_iota(jnp.int32, (rows, 128), 1)

        def mean_factor(held, base):
            comp = jnp.zeros((rows, 128), jnp.float32)
            for x in range(nx):
                part = wts[x] * (1.0 - held[base + x, 0:rows, :])
                comp = jnp.where(lane == x, jnp.sum(part, axis=1, keepdims=True), comp)
            return 1.0 + 0.3 * jnp.tanh(comp)

        st_away.wait_recv()
        st_keep.wait()
        const_arrive((0, 1))
        all_faces()
        const_arrive((2,))
        lax.fori_loop(1, ex - 1, first, 0, unroll=2)
        relax(ta, tb, 2, ey)
        relax(tb, ta, 3, ey)
        relax(ta, px0, 4, rows)
        push(0, px0)
        lax.fori_loop(0, nx, reduce_columns, 0)
        for group in ((0, 1), (2,)):
            const_each(group, lambda c: c.wait_send(), None)
        st_away.wait_send()
        arrive(0, px0)
        relax(px0, ta, 1, ey)
        relax(ta, tb, 2, ey)
        relax(tb, ta, 3, ey)
        relax(ta, px1, 4, rows)

        factor = mean_factor(px1, W)
        cols[1, 0:rows, :] = factor
        push(2, cols)
        push(1, px1)
        sent(0, px0)
        arrive(2, cols)
        for x in range(ex):
            part, pos = (0, x + nx - W) if x < W else ((1, x - W) if x < W + nx else (2, x - W - nx))
            t = cols[part, :, pos:pos + 1]
            k_ext[x] = k_ext[x] * (t * t * t)
        all_faces()
        arrive(1, px1)
        relax(px1, ta, 1, ey)
        relax(ta, tb, 2, ey)
        relax(tb, ta, 3, ey)
        relax(ta, px2, 4, rows)
        push(3, px2)
        sent(2, cols)
        sent(1, px1)
        arrive(3, px2)
        relax(px2, ta, 1, ey)
        relax(ta, tb, 2, ey)
        relax(tb, ta, 3, ey)
        relax(ta, fin_p, 4, rows)

        def give(n, ref, dst, x0, xn):
            out = pltpu.make_async_remote_copy(
                ref.at[pl.ds(x0, xn), :, pl.ds(z_there, nz)], dst.at[pl.ds(x0, xn), pl.ds(mine, rows), :],
                psend.at[n], precv.at[n], device_id={"grp": other}, device_id_type=MESH)
            keep = pltpu.make_async_copy(
                ref.at[pl.ds(x0, xn), :, pl.ds(z_here, nz)], dst.at[pl.ds(x0, xn), pl.ds(mine, rows), :],
                loc.at[2 + n])
            return out, keep

        half = nx // 2
        gives = [give(1, fin_p, p_out, 0, nx), give(2, fin_d, d_out, 0, half), give(3, fin_d, d_out, half, half)]
        for c in gives[0]:
            c.start()

        def solve_columns(x, carry):
            r = 0.001 * (1.0 - fin_p[x])
            for level in range(levels):
                stride = 1 << level
                r = (r + alpha[level, x] * pltpu.roll(r, stride, 1)
                     + gamma[level, x] * pltpu.roll(r, depth - stride, 1))
            fin_d[x] = r * inv[x]
            return carry

        for n in range(2):
            lax.fori_loop(n * half, (n + 1) * half, solve_columns, 0, unroll=half)
            for c in gives[1 + n]:
                c.start()

        factor = factor * mean_factor(fin_p, 0)
        spot = lane == lax.broadcasted_iota(jnp.int32, (rows, 128), 0) + g * rows
        pick = lax.broadcasted_iota(jnp.int32, (nx, 128), 0)
        mixed = jnp.zeros((nx, 128), jnp.float32)
        for x in range(nx):
            row = jnp.sum(jnp.where(spot, factor[:, x:x + 1], 0.0), axis=0, keepdims=True)
            mixed = jnp.where(pick == x, row, mixed)
        line[...] = mixed
        t_out = pltpu.make_async_remote_copy(
            line, line_in, psend.at[4], precv.at[4], device_id={"grp": other}, device_id_type=MESH)
        t_out.start()
        sent(3, px2)
        for out, keep in gives:
            out.wait_send()
            keep.wait()
        t_out.wait_send()
        t_out.wait_recv()
        th_out[...] = thick[...] * (mixed + line_in[...])[:, 0:ny]
        for out, keep in gives:
            out.wait_recv()

    return kernel, rows, depth, ex, ey, levels


def body(source, fill, material, thickness, perm_table, stiff_table):
    nx, ny, nz = source.shape
    kernel, rows, depth, ex, ey, levels = make_kernel(
        nx, ny, nz, lax.axis_size("gx"), lax.axis_size("gy"), perm_table.shape[0])
    f32, i32 = jnp.float32, jnp.int32
    vm = pl.BlockSpec(memory_space=pltpu.VMEM)
    hb = pl.BlockSpec(memory_space=pl.ANY)
    hbm = pl.BlockSpec(memory_space=pltpu.HBM)
    ext = pltpu.VMEM((ex, ey, depth), f32)
    iext = pltpu.VMEM((ex, ey, depth), i32)
    own = pltpu.VMEM((nx, rows, depth), f32)
    brick = pltpu.VMEM((nx, ny, nz), f32)
    dma = pltpu.SemaphoreType.DMA
    return pl.pallas_call(
        kernel,
        out_shape=(
            jax.ShapeDtypeStruct((nx, ny, nz), f32),
            jax.ShapeDtypeStruct((nx, ny, nz), f32),
            jax.ShapeDtypeStruct((nx, ny), f32),
        ),
        in_specs=[hbm] * 6,
        out_specs=(hb, hb, vm),
        scratch_shapes=[
            ext, iext, ext, ext, ext, ext, ext, ext, ext, ext, ext, ext,
            pltpu.VMEM((levels, nx, rows, depth), f32),
            pltpu.VMEM((levels, nx, rows, depth), f32),
            own, own,
            pltpu.VMEM((3, ey, 128), f32),
            own, own,
            pltpu.VMEM((nx, ny, nz), i32), brick, brick, own,
            pltpu.VMEM((nx, ny), f32),
            pltpu.VMEM((nx, 128), f32),
            pltpu.VMEM((nx, 128), f32),
            pltpu.SMEM(perm_table.shape, f32), pltpu.SMEM(stiff_table.shape, f32),
            dma((3, 2, 9)), dma((3, 2, 9)), dma((3, 2)),
            dma((4, 8)), dma((4, 8)), dma((5,)), dma((5,)), dma((8,)),
        ],
        compiler_params=pltpu.CompilerParams(
            collective_id=0, has_side_effects=True, vmem_limit_bytes=VMEM_LIMIT),
    )(*(pltpu.with_memory_space_constraint(a, pltpu.HBM)
        for a in (source, fill, material, thickness, perm_table, stiff_table)))


def solution(mesh):
    return jax.shard_map(
        body,
        mesh=mesh,
        in_specs=(
            P("gx", "gy", "grp"),
            P("gx", "gy", "grp"),
            P("gx", "gy", "grp"),
            P("gx", "gy"),
            P(),
            P(),
        ),
        out_specs=(P("gx", "gy", "grp"), P("gx", "gy", "grp"), P("gx", "gy")),
        check_vma=False,
    )
```

time: 69.5 us -> 55 us (0.79)
  Pallas kernels: 65 us -> 52.1 us
  local copies, waits for them, and re-layouts: 3.64 us -> 1.9 us
    pallas_call x1, Pallas kernels: 65 us -> 52.1 us  [body(): pl.pallas_call(kernel, out_shape=(jax.ShapeDtypeStruct((nx, ny, nz), f32)...]
    unnamed x5 -> x3, local copies, waits for them, and re-layouts: 2.92 us -> 1.9 us
    transpose x1 -> x0, local copies, waits for them, and re-layouts: 0.72 us -> none  [body(): return (pressure, disp, thick[:, :nx].T)]
where the time goes in v1:
time: 55 us; the launch traced here: 54.7 us
  Pallas kernels  52.1 us (95%)
  local copies, waits for them, and re-layouts  1.9 us (3%)
  between operations  0.64 us (1%)
    pallas_call x1, Pallas kernels, body(): pl.pallas_call(kernel, out_shape=(jax.ShapeDtypeStruct((nx, ny, nz), f32)...  52.1 us
    unnamed x3, local copies, waits for them, and re-layouts  1.9 us

profile of v1, /device:TPU:47, one launch (start us, length us, event | category | flops | bytes accessed | tf_op | source)
XLA Modules:
  0.0 54.7 jit_solution(10260271553695074186)
XLA Ops:
  0.6 52.1 %shard_map.85 = (f32[8,32,128]{2,1,0:T(8,128)S(1)}, f32[8,32,128]{2,1,0:T(8,128)S(1)}, f32[8,32]{1,0:T(8,128)S(1)}) custom-call(f32[8,32,128]{2,1,0:T(8,128)} %source.1, s32[8,32,128]{2,1,0:T(8,128)} %fill.1, s32[8,32,128]{2,1,0:T(8,128)} %material.1, f32[8,32]{1,0:T(8,128)} %thickness.1, f32[8]{0:T(128)} %perm_table.1, f32[8]{0:T(128)} %stiff_table.1), custom_call_target="tpu_custom_call" | custom-call | tf_op jit(solution)/shard_map/pallas_call | solution.py:413
  52.8 0.7 %copy.12 = f32[8,32,128]{2,1,0:T(8,128)} copy(f32[8,32,128]{2,1,0:T(8,128)S(1)} %get-tuple-element.6) | data formatting | bytes 262144
  53.4 0.7 %copy.13 = f32[8,32,128]{2,1,0:T(8,128)} copy(f32[8,32,128]{2,1,0:T(8,128)S(1)} %get-tuple-element.7) | data formatting | bytes 262144
  54.1 0.6 %copy.14 = f32[8,32]{1,0:T(8,128)} copy(f32[8,32]{1,0:T(8,128)S(1)} %get-tuple-element.8) | data formatting | bytes 2048

commit v2 on v1

--- a/solution.py
+++ b/solution.py
@@ -34,6 +34,14 @@
         ys, yd = {-1: ((0, yr), (rows, yr)), 0: ((0, rows), (0, rows)),
                   1: ((rows - yr, yr), (ey - yr, yr))}[dy]
         return xs, ys, xd, yd
+
+    def blocks_for(dx, dy, reach):
+        _, (ys, yn), _, (yd, _) = blocks(0, dy, reach)
+        xr = reach - abs(dy)
+        yn, ys, yd = (yn, ys, yd) if dy == 0 else (reach - 1, ys + (1 if dy == 1 else 0), yd + (1 if dy == 1 else 0))
+        xs = jnp.where(dx == -1, 0, nx - xr)
+        xd = jnp.where(dx == -1, W + nx, W - xr)
+        return (xs, xr), (ys, yn), (xd, xr), (yd, yn)
 
     def kernel(source, fill, material, thickness, perm_table, stiff_table, p_out, d_out, th_out,
                s_ext, f_ext, k_ext, px0, px1, px2, ta, tb, gx_, gy_, gz_, a_,
@@ -43,6 +51,7 @@
         ix = lax.axis_index("gx")
         iy = lax.axis_index("gy")
         slab = 2 * iy + g
+        far = jnp.where(lax.rem(ix, 4) < 2, -1, 1)
         other = 1 - g
 
         def within(value, count):
@@ -50,17 +59,18 @@
 
         def place(dx, dy):
             x = jnp.clip(ix + dx, 0, ngx - 1)
-            s = jnp.clip(slab + dy, 0, nslab - 1)
-            return {"grp": lax.rem(s, 2), "gx": x, "gy": lax.div(s, 2)}
+            if dy == 0:
+                return {"grp": g, "gx": x, "gy": iy}
+            return {"grp": other, "gx": x, "gy": jnp.clip(iy + (g if dy == 1 else g - 1), 0, ngy - 1)}
 
         alive = [within(ix + dx, ngx) * within(slab + dy, nslab) for dx, dy in DIRS]
 
         barrier = pltpu.get_barrier_semaphore()
-        for dx in (-1, 0, 1):
-            for dgy in (0, 2 * g - 1):
+        for dx in (far, 0, -far):
+            for dgy in (2 * g - 1, 0):
                 for core in range(2):
                     ok = within(ix + dx, ngx) * within(iy + dgy, ngy)
-                    if dx == 0 and isinstance(dgy, int):
+                    if isinstance(dx, int) and isinstance(dgy, int):
                         ok = jnp.where(g == core, 0, 1)
 
                     @pl.when(ok == 1)
@@ -109,37 +119,44 @@
         z_there = pl.multiple_of(other * nz, nz)
         consts = [(0, kloc, k_ext, W), (1, fill, f_ext, W - 1), (2, source, s_ext, W - 1)]
 
-        def const_send(n, v, i, local=False):
+        def const_send(n, v, dx, dy, local=False):
             _, src, ext, reach = consts[n]
-            dx, dy = NINE[i]
-            (xs, xn), (ys, yn), (xd, _), (yd, _) = blocks(dx, dy, reach)
+            if dx is None:
+                (xs, xn), (ys, yn), (xd, _), (yd, _) = blocks(0, dy, reach)
+                i, x = NINE.index((0, dy)), ix
+            else:
+                (xs, xn), (ys, yn), (xd, _), (yd, _) = blocks_for(dx, dy, reach)
+                i, x = jnp.where(dx == -1, 2, 7) + dy, jnp.clip(ix + dx, 0, ngx - 1)
             core, dgy = (v + dy) % 2, (v + dy) // 2
             from_ = src.at[pl.ds(xs, xn), pl.ds(v * rows + ys, yn), :]
             to = ext.at[pl.ds(xd, xn), pl.ds(yd, yn), pl.ds(z_here, nz)]
-            target = {"grp": core, "gx": jnp.clip(ix + dx, 0, ngx - 1), "gy": jnp.clip(iy + dgy, 0, ngy - 1)}
+            target = {"grp": core, "gx": x, "gy": jnp.clip(iy + dgy, 0, ngy - 1)}
             if local:
                 return pltpu.make_async_copy(from_, to, cloc.at[n, 0 if dy == 0 else 1])
             return pltpu.make_async_remote_copy(
                 from_, to, csend.at[n, v, i], crecv.at[n, g, i], device_id=target, device_id_type=MESH)
 
-        def const_each(group, do_away, do_keep):
-            for v in range(2):
-                for i in range(9):
-                    dx, dy = NINE[i]
-                    core, dgy = (v + dy) % 2, (v + dy) // 2
-                    ok = within(ix + dx, ngx) * within(iy + dgy, ngy)
-                    if dx == 0 and dgy == 0:
-                        ok = jnp.where(g == core, 0, 1)
-                        if do_keep is not None:
-                            @pl.when(g == core)
-                            def _():
-                                for n in group:
-                                    do_keep(const_send(n, v, i, True))
-
-                    @pl.when(ok == 1)
-                    def _():
-                        for n in group:
-                            do_away(const_send(n, v, i))
+        def const_each(do_away, do_keep):
+            for dx in (far, None, -far):
+                for v in range(2):
+                    for dy in (0, 1, -1):
+                        core, dgy = (v + dy) % 2, (v + dy) // 2
+                        if dx is None:
+                            ok = within(iy + dgy, ngy)
+                            if dgy == 0:
+                                ok = jnp.where(g == core, 0, 1)
+                                if do_keep is not None:
+                                    @pl.when(g == core)
+                                    def _():
+                                        for n in range(3):
+                                            do_keep(const_send(n, v, dx, dy, True))
+                        else:
+                            ok = within(ix + dx, ngx) * within(iy + dgy, ngy)
+
+                        @pl.when(ok == 1)
+                        def _():
+                            for n in range(3):
+                                do_away(const_send(n, v, dx, dy))
 
         def const_arrive(group):
             for src in range(2):
@@ -182,8 +199,7 @@
             stloc.at[:, pl.ds(mine, rows), :], st.at[:, :, pl.ds(z_here, nz)], loc.at[2])
         st_away.start()
         st_keep.start()
-        for group in ((0, 1), (2,)):
-            const_each(group, lambda c: c.start(), lambda c: c.start())
+        const_each(lambda c: c.start(), lambda c: c.start())
 
         def hop(e, ref, i):
             dx, dy = DIRS[i]
@@ -198,10 +214,27 @@
                 src, dst, send.at[e, i], recv.at[e, i], device_id=place(dx, dy), device_id_type=MESH)
 
         def push(e, ref):
-            for i in ORDER:
-                @pl.when(alive[i] == 1)
-                def _():
-                    hop(e, ref, i).start()
+            for dx in (far, None, -far):
+                for dy in ((0, 1, -1) if dx is not None else (1, -1)):
+                    if dx is None:
+                        (xs, xn), (ys, yn), (xd, _), (yd, _) = blocks(0, dy, W)
+                        i, x, into = DIRS.index((0, dy)), ix, 1
+                    else:
+                        (xs, xn), (ys, yn), (xd, _), (yd, _) = blocks_for(dx, dy, W)
+                        i, x, into = jnp.where(dx == -1, 1, 6) + dy, jnp.clip(ix + dx, 0, ngx - 1), 1 - dx
+                    if ref is cols:
+                        src, dst = ref.at[1, pl.ds(ys, yn), :], ref.at[into, pl.ds(yd, yn), :]
+                    else:
+                        src = ref.at[pl.ds(W + xs, xn), pl.ds(ys, yn), :]
+                        dst = ref.at[pl.ds(xd, xn), pl.ds(yd, yn), :]
+                    target = place(0, dy)
+                    target["gx"] = x
+                    ok = within(x if dx is None else ix + dx, ngx) * within(slab + dy, nslab)
+
+                    @pl.when(ok == 1)
+                    def _():
+                        pltpu.make_async_remote_copy(
+                            src, dst, send.at[e, i], recv.at[e, i], device_id=target, device_id_type=MESH).start()
 
         def arrive(e, ref):
             for i in range(8):
@@ -311,8 +344,7 @@
         relax(ta, px0, 4, rows)
         push(0, px0)
         lax.fori_loop(0, nx, reduce_columns, 0)
-        for group in ((0, 1), (2,)):
-            const_each(group, lambda c: c.wait_send(), None)
+        const_each(lambda c: c.wait_send(), None)
         st_away.wait_send()
         arrive(0, px0)
         relax(px0, ta, 1, ey)
@@ -410,7 +442,7 @@
     own = pltpu.VMEM((nx, rows, depth), f32)
     brick = pltpu.VMEM((nx, ny, nz), f32)
     dma = pltpu.SemaphoreType.DMA
-    return pl.pallas_call(
+    fields = pl.pallas_call(
         kernel,
         out_shape=(
             jax.ShapeDtypeStruct((nx, ny, nz), f32),
@@ -439,6 +471,23 @@
     )(*(pltpu.with_memory_space_constraint(a, pltpu.HBM)
         for a in (source, fill, material, thickness, perm_table, stiff_table)))
 
+    def settle(*refs):
+        ins, outs, sems = refs[:3], refs[3:6], refs[6]
+        copies = [pltpu.make_async_copy(i, o, sems.at[n]) for n, (i, o) in enumerate(zip(ins, outs))]
+        for c in copies:
+            c.start()
+        for c in copies:
+            c.wait()
+
+    return pl.pallas_call(
+        settle,
+        out_shape=tuple(jax.ShapeDtypeStruct(a.shape, f32) for a in fields),
+        in_specs=[hb] * 3,
+        out_specs=(hbm,) * 3,
+        scratch_shapes=[dma((3,))],
+        compiler_params=pltpu.CompilerParams(vmem_limit_bytes=1 << 20),
+    )(*fields)
+
 
 def solution(mesh):
     return jax.shard_map(

time: 55 us -> 52 us (0.945)
  local copies, waits for them, and re-layouts: 1.9 us -> 0 us
  Pallas kernels: 52.1 us -> 51.2 us
    unnamed x3 -> x0, local copies, waits for them, and re-layouts: 1.9 us -> none
    pallas_call x1, Pallas kernels: 52.1 us -> 50.5 us  [body(): pl.pallas_call(kernel, out_shape=(jax.ShapeDtypeStruct((nx, ny, nz), f32)...]
    pallas_call x0 -> x1, Pallas kernels: none -> 0.73 us  [body(): pl.pallas_call(settle, out_shape=tuple((jax.ShapeDtypeStruct(a.shape, f32...]
where the time goes in v2:
time: 52 us; the launch traced here: 51.9 us
  Pallas kernels  51.2 us (98%)
  between operations  0.64 us (1%)
    pallas_call x1, Pallas kernels, body(): pl.pallas_call(kernel, out_shape=(jax.ShapeDtypeStruct((nx, ny, nz), f32)...  50.5 us

profile of v2, /device:TPU:47, one launch (start us, length us, event | category | flops | bytes accessed | tf_op | source)
XLA Modules:
  0.0 51.9 jit_solution(6520934887429320066)
XLA Ops:
  0.6 50.5 %shard_map.85 = (f32[8,32,128]{2,1,0:T(8,128)S(1)}, f32[8,32,128]{2,1,0:T(8,128)S(1)}, f32[8,32]{1,0:T(8,128)S(1)}) custom-call(f32[8,32,128]{2,1,0:T(8,128)} %source.1, s32[8,32,128]{2,1,0:T(8,128)} %fill.1, s32[8,32,128]{2,1,0:T(8,128)} %material.1, f32[8,32]{1,0:T(8,128)} %thickness.1, f32[8]{0:T(128)} %perm_table.1, f32[8]{0:T(128)} %stiff_table.1), custom_call_target="tpu_custom_call" | custom-call | tf_op jit(solution)/shard_map/pallas_call | solution.py:445
  51.2 0.7 %shard_map.86 = (f32[8,32,128]{2,1,0:T(8,128)}, f32[8,32,128]{2,1,0:T(8,128)}, f32[8,32]{1,0:T(8,128)}) custom-call(f32[8,32,128]{2,1,0:T(8,128)S(1)} %get-tuple-element.6.refs_0_, f32[8,32,128]{2,1,0:T(8,128)S(1)} %get-tuple-element.7.refs_1_, f32[8,32]{1,0:T(8,128)S(1)} %get-tuple-element.8.refs_2_), custom_call_target="tpu_custom_call" | custom-call | tf_op jit(solution)/shard_map/pallas_call | solution.py:482

commit v3 on v2

--- a/solution.py
+++ b/solution.py
@@ -11,7 +11,7 @@
 DIRS = [(-1, -1), (-1, 0), (-1, 1), (0, -1), (0, 1), (1, -1), (1, 0), (1, 1)]
 NINE = [(0, 0)] + DIRS
 ORDER = [0, 1, 2, 3, 4, 5, 6, 7]
-FACES = 2
+FACES = 14
 
 
 def spread(table, material, count):
@@ -214,7 +214,7 @@
                 src, dst, send.at[e, i], recv.at[e, i], device_id=place(dx, dy), device_id_type=MESH)
 
         def push(e, ref):
-            for dx in (far, None, -far):
+            for dx in (None, far, -far):
                 for dy in ((0, 1, -1) if dx is not None else (1, -1)):
                     if dx is None:
                         (xs, xn), (ys, yn), (xd, _), (yd, _) = blocks(0, dy, W)
@@ -400,8 +400,8 @@
             fin_d[x] = r * inv[x]
             return carry
 
+        lax.fori_loop(0, nx, solve_columns, 0, unroll=nx)
         for n in range(2):
-            lax.fori_loop(n * half, (n + 1) * half, solve_columns, 0, unroll=half)
             for c in gives[1 + n]:
                 c.start()
 

time: 52 us -> 50.6 us (0.973)
  Pallas kernels: 51.2 us -> 49.8 us
    pallas_call x1, Pallas kernels: 50.5 us -> 49.1 us  [body(): pl.pallas_call(kernel, out_shape=(jax.ShapeDtypeStruct((nx, ny, nz), f32)...]
where the time goes in v3:
time: 50.6 us; the launch traced here: 50.4 us
  Pallas kernels  49.8 us (98%)
  between operations  0.64 us (1%)
    pallas_call x1, Pallas kernels, body(): pl.pallas_call(kernel, out_shape=(jax.ShapeDtypeStruct((nx, ny, nz), f32)...  49.1 us

profile of v3, /device:TPU:47, one launch (start us, length us, event | category | flops | bytes accessed | tf_op | source)
XLA Modules:
  0.0 50.4 jit_solution(6538168511056775248)
XLA Ops:
  0.6 49.1 %shard_map.85 = (f32[8,32,128]{2,1,0:T(8,128)S(1)}, f32[8,32,128]{2,1,0:T(8,128)S(1)}, f32[8,32]{1,0:T(8,128)S(1)}) custom-call(f32[8,32,128]{2,1,0:T(8,128)} %source.1, s32[8,32,128]{2,1,0:T(8,128)} %fill.1, s32[8,32,128]{2,1,0:T(8,128)} %material.1, f32[8,32]{1,0:T(8,128)} %thickness.1, f32[8]{0:T(128)} %perm_table.1, f32[8]{0:T(128)} %stiff_table.1), custom_call_target="tpu_custom_call" | custom-call | tf_op jit(solution)/shard_map/pallas_call | solution.py:445
  49.7 0.7 %shard_map.86 = (f32[8,32,128]{2,1,0:T(8,128)}, f32[8,32,128]{2,1,0:T(8,128)}, f32[8,32]{1,0:T(8,128)}) custom-call(f32[8,32,128]{2,1,0:T(8,128)S(1)} %get-tuple-element.6.refs_0_, f32[8,32,128]{2,1,0:T(8,128)S(1)} %get-tuple-element.7.refs_1_, f32[8,32]{1,0:T(8,128)S(1)} %get-tuple-element.8.refs_2_), custom_call_target="tpu_custom_call" | custom-call | tf_op jit(solution)/shard_map/pallas_call | solution.py:482

commit v4 on v3

--- a/solution.py
+++ b/solution.py
@@ -343,9 +343,7 @@
         relax(tb, ta, 3, ey)
         relax(ta, px0, 4, rows)
         push(0, px0)
-        lax.fori_loop(0, nx, reduce_columns, 0)
-        const_each(lambda c: c.wait_send(), None)
-        st_away.wait_send()
+        lax.fori_loop(0, nx, reduce_columns, 0, unroll=2)
         arrive(0, px0)
         relax(px0, ta, 1, ey)
         relax(ta, tb, 2, ey)
@@ -371,6 +369,8 @@
         push(3, px2)
         sent(2, cols)
         sent(1, px1)
+        const_each(lambda c: c.wait_send(), None)
+        st_away.wait_send()
         arrive(3, px2)
         relax(px2, ta, 1, ey)
         relax(ta, tb, 2, ey)

time: 50.6 us -> 50.5 us (level)
  no operation moved by 1% of the time
where the time goes in v4:
time: 50.5 us; the launch traced here: 50.4 us
  Pallas kernels  49.8 us (99%)
  between operations  0.64 us (1%)
    pallas_call x1, Pallas kernels, body(): pl.pallas_call(kernel, out_shape=(jax.ShapeDtypeStruct((nx, ny, nz), f32)...  49 us

profile of v4, /device:TPU:47, one launch (start us, length us, event | category | flops | bytes accessed | tf_op | source)
XLA Modules:
  0.0 50.4 jit_solution(4817172491597172143)
XLA Ops:
  0.6 49.0 %shard_map.85 = (f32[8,32,128]{2,1,0:T(8,128)S(1)}, f32[8,32,128]{2,1,0:T(8,128)S(1)}, f32[8,32]{1,0:T(8,128)S(1)}) custom-call(f32[8,32,128]{2,1,0:T(8,128)} %source.1, s32[8,32,128]{2,1,0:T(8,128)} %fill.1, s32[8,32,128]{2,1,0:T(8,128)} %material.1, f32[8,32]{1,0:T(8,128)} %thickness.1, f32[8]{0:T(128)} %perm_table.1, f32[8]{0:T(128)} %stiff_table.1), custom_call_target="tpu_custom_call" | custom-call | tf_op jit(solution)/shard_map/pallas_call | solution.py:445
  49.7 0.7 %shard_map.86 = (f32[8,32,128]{2,1,0:T(8,128)}, f32[8,32,128]{2,1,0:T(8,128)}, f32[8,32]{1,0:T(8,128)}) custom-call(f32[8,32,128]{2,1,0:T(8,128)S(1)} %get-tuple-element.6.refs_0_, f32[8,32,128]{2,1,0:T(8,128)S(1)} %get-tuple-element.7.refs_1_, f32[8,32]{1,0:T(8,128)S(1)} %get-tuple-element.8.refs_2_), custom_call_target="tpu_custom_call" | custom-call | tf_op jit(solution)/shard_map/pallas_call | solution.py:482

commit v5 on v4

--- a/solution.py
+++ b/solution.py
@@ -52,6 +52,7 @@
         iy = lax.axis_index("gy")
         slab = 2 * iy + g
         far = jnp.where(lax.rem(ix, 4) < 2, -1, 1)
+        long_way = jnp.where(lax.rem(ix, 4) == 0, 1, 0) + jnp.where(lax.rem(ix, 4) == 3, 1, 0)
         other = 1 - g
 
         def within(value, count):
@@ -213,28 +214,36 @@
             return pltpu.make_async_remote_copy(
                 src, dst, send.at[e, i], recv.at[e, i], device_id=place(dx, dy), device_id_type=MESH)
 
-        def push(e, ref):
-            for dx in (None, far, -far):
-                for dy in ((0, 1, -1) if dx is not None else (1, -1)):
-                    if dx is None:
-                        (xs, xn), (ys, yn), (xd, _), (yd, _) = blocks(0, dy, W)
-                        i, x, into = DIRS.index((0, dy)), ix, 1
-                    else:
-                        (xs, xn), (ys, yn), (xd, _), (yd, _) = blocks_for(dx, dy, W)
-                        i, x, into = jnp.where(dx == -1, 1, 6) + dy, jnp.clip(ix + dx, 0, ngx - 1), 1 - dx
-                    if ref is cols:
-                        src, dst = ref.at[1, pl.ds(ys, yn), :], ref.at[into, pl.ds(yd, yn), :]
-                    else:
-                        src = ref.at[pl.ds(W + xs, xn), pl.ds(ys, yn), :]
-                        dst = ref.at[pl.ds(xd, xn), pl.ds(yd, yn), :]
-                    target = place(0, dy)
-                    target["gx"] = x
-                    ok = within(x if dx is None else ix + dx, ngx) * within(slab + dy, nslab)
-
-                    @pl.when(ok == 1)
-                    def _():
-                        pltpu.make_async_remote_copy(
-                            src, dst, send.at[e, i], recv.at[e, i], device_id=target, device_id_type=MESH).start()
+        def push_one(e, ref, dx, dy, cond):
+            if dx is None:
+                (xs, xn), (ys, yn), (xd, _), (yd, _) = blocks(0, dy, W)
+                i, x, into = DIRS.index((0, dy)), ix, 1
+            else:
+                (xs, xn), (ys, yn), (xd, _), (yd, _) = blocks_for(dx, dy, W)
+                i, x, into = jnp.where(dx == -1, 1, 6) + dy, jnp.clip(ix + dx, 0, ngx - 1), 1 - dx
+            if ref is cols:
+                src, dst = ref.at[1, pl.ds(ys, yn), :], ref.at[into, pl.ds(yd, yn), :]
+            else:
+                src = ref.at[pl.ds(W + xs, xn), pl.ds(ys, yn), :]
+                dst = ref.at[pl.ds(xd, xn), pl.ds(yd, yn), :]
+            target = place(0, dy)
+            target["gx"] = x
+            ok = within(x if dx is None else ix + dx, ngx) * within(slab + dy, nslab) * cond
+
+            @pl.when(ok == 1)
+            def _():
+                pltpu.make_async_remote_copy(
+                    src, dst, send.at[e, i], recv.at[e, i], device_id=target, device_id_type=MESH).start()
+
+        def push(e, ref, pause=None):
+            for dy in (1, -1):
+                push_one(e, ref, None, dy, 1)
+            if pause:
+                pause()
+            for dy in (0, 1, -1):
+                push_one(e, ref, far, dy, 1)
+            for dy in (0, 1, -1):
+                push_one(e, ref, -far, dy, 1)
 
         def arrive(e, ref):
             for i in range(8):
@@ -350,10 +359,15 @@
         relax(tb, ta, 3, ey)
         relax(ta, px1, 4, rows)
 
-        factor = mean_factor(px1, W)
-        cols[1, 0:rows, :] = factor
-        push(2, cols)
-        push(1, px1)
+        held = []
+
+        def columns():
+            held.append(mean_factor(px1, W))
+            cols[1, 0:rows, :] = held[0]
+            push(2, cols)
+
+        push(1, px1, columns)
+        factor = held[0]
         sent(0, px0)
         arrive(2, cols)
         for x in range(ex):

time: 50.5 us -> 50.5 us (level)
  no operation moved by 1% of the time
where the time goes in v5:
time: 50.5 us; the launch traced here: 50.4 us
  Pallas kernels  49.7 us (98%)
  between operations  0.64 us (1%)
    pallas_call x1, Pallas kernels, body(): pl.pallas_call(kernel, out_shape=(jax.ShapeDtypeStruct((nx, ny, nz), f32)...  49 us

profile of v5, /device:TPU:47, one launch (start us, length us, event | category | flops | bytes accessed | tf_op | source)
XLA Modules:
  0.0 50.4 jit_solution(7087294542710027951)
XLA Ops:
  0.6 49.0 %shard_map.85 = (f32[8,32,128]{2,1,0:T(8,128)S(1)}, f32[8,32,128]{2,1,0:T(8,128)S(1)}, f32[8,32]{1,0:T(8,128)S(1)}) custom-call(f32[8,32,128]{2,1,0:T(8,128)} %source.1, s32[8,32,128]{2,1,0:T(8,128)} %fill.1, s32[8,32,128]{2,1,0:T(8,128)} %material.1, f32[8,32]{1,0:T(8,128)} %thickness.1, f32[8]{0:T(128)} %perm_table.1, f32[8]{0:T(128)} %stiff_table.1), custom_call_target="tpu_custom_call" | custom-call | tf_op jit(solution)/shard_map/pallas_call | solution.py:459
  49.6 0.7 %shard_map.86 = (f32[8,32,128]{2,1,0:T(8,128)}, f32[8,32,128]{2,1,0:T(8,128)}, f32[8,32]{1,0:T(8,128)}) custom-call(f32[8,32,128]{2,1,0:T(8,128)S(1)} %get-tuple-element.6.refs_0_, f32[8,32,128]{2,1,0:T(8,128)S(1)} %get-tuple-element.7.refs_1_, f32[8,32]{1,0:T(8,128)S(1)} %get-tuple-element.8.refs_2_), custom_call_target="tpu_custom_call" | custom-call | tf_op jit(solution)/shard_map/pallas_call | solution.py:496
